TPU v7x, 256 devices: a whole 4x4x8 slice. The times are simulated.
256 devices in a mesh: tx: 4 (over z_lo, core), img: 64 (over y, z_hi, x).
Axes of the slice: x: 4, y: 4, z: 8 (z_hi: 4, z_lo: 2; z = z_hi * 2 + z_lo), core: 2. Of those that a mesh axis runs over, the one named last changes fastest.
Arguments:
- encoded: bfloat16 [1024, 1024, 512], P('tx', 'img'), may hold values from -6 to 6
- signs: int32 [1024, 64], replicated, may hold values from -1 to 1, as said below
- tx_block: int32 [64, 16384], P('tx'), may hold values from 0 to 1
- rx_block: int32 [1024, 16384], P(None, 'img'), may hold values from 0 to 2
- apodization: int32 [1024, 16384], P(None, 'img'), may hold values 0 or 1
Outputs:
- image: float32 [16384, 128], P('img', 'tx')
Inputs may be any that keep to these rules, and one draw needn't show every extreme that they name: `signs`: every entry is 1 or -1. The columns are 64 distinct columns of the Sylvester Hadamard matrix of order 1024, every row multiplied by its own sign, so that two different columns are orthogonal.
All inputs are finite; a program needn't handle non-finite values. No bound on the sum of `apodization` on one device may be relied on, other than what follows from the above.
Results may differ from a plain program's by a relative error of at most 0.0029.
Values may be sent and summed in bfloat16 or wider, within the bound.
A program may use at most 192 MiB of HBM per device.

v0:
```python
import math
import jax
import jax.numpy as jnp
from jax import lax
from jax.sharding import PartitionSpec as P

E = 1024
K = 64
R = 1024
L = 128


def weights_for(rx_rows, mask_rows, tx_rows, block_count):
    total_block = tx_rows.T[:, :, None] + rx_rows.T[:, None, :]
    levels = jnp.arange(block_count, dtype=jnp.int32)
    chosen = total_block[..., None] == levels
    weight = jnp.where(
        chosen, mask_rows.T[:, None, :, None].astype(jnp.bfloat16), jnp.zeros((), jnp.bfloat16)
    )
    return weight.reshape(weight.shape[0], -1)


def on_device(encoded, signs, tx_block, rx_block, apodization):
    events_here, receivers_here, sample_count = encoded.shape
    transmits_here = tx_block.shape[0]
    lines_here = rx_block.shape[1]
    block_count = sample_count // L
    tx_index = lax.axis_index("tx")
    img_index = lax.axis_index("img")
    sign_cols = lax.dynamic_slice_in_dim(
        signs, tx_index * transmits_here, transmits_here, 1
    ).astype(jnp.bfloat16)
    piece = lax.all_gather(encoded, "tx", axis=0, tiled=True)
    flat_piece = piece.reshape(piece.shape[0], -1)
    summed = lax.dot_general(
        sign_cols, flat_piece, (((0,), (0,)), ((), ())), preferred_element_type=jnp.float32
    )
    decoded = (
        (summed * (1.0 / E))
        .astype(jnp.bfloat16)
        .reshape(transmits_here, receivers_here, sample_count)
    )
    own_tx = lax.dynamic_slice_in_dim(tx_block, img_index * lines_here, lines_here, 1)
    weight = weights_for(rx_block, apodization, own_tx, block_count)
    image = jnp.dot(
        weight,
        lax.all_gather(decoded, "img", axis=1, tiled=True).reshape(-1, L),
        preferred_element_type=jnp.float32,
    )
    scale = math.sqrt(E / (K * R))
    return lax.psum_scatter(image * scale, "tx", scatter_dimension=1, tiled=True)


def solution(mesh):
    placed = (P("tx", "img", None), P(), P("tx", None), P(None, "img"), P(None, "img"))
    return jax.shard_map(
        on_device, mesh=mesh, in_specs=placed, out_specs=P("img", "tx"), check_vma=False
    )
```

profile of v0, /device:TPU:1, one launch (start us, length us, event | category | flops | bytes accessed | tf_op | source)
XLA Modules:
  0.0 436.7 jit_solution(3269793722373958199)
XLA Ops:
  6.5 0.0 copy-start
  6.5 0.0 all-gather.3.cloned.1.call-start
  6.5 0.7 all-gather.3.cloned.1.call-update
  7.3 0.0 all-gather.5.cloned.1.call-start
  7.3 159.8 %all-gather.3.cloned.1.call-done = bf16[1024,16,512]{2,1,0:T(8,128)(2,1)} async-done(((bf16[256,16,512]{2,1,0:T(8,128)(2,1)}), bf16[1024,16,512]{2,1,0:T(8,128)(2,1)}) %all-gather.3.cloned.1.call-update) | async-done | bytes 16777232 | tf_op jit(solution)/shard_map/all_gather | solution.py:33
  167.1 15.8 %copy.9 = bf16[128,8,16,512]{3,1,2,0:T(8,128)(2,1)S(1)} copy(bf16[128,8,16,512]{3,2,1,0:T(8,128)(2,1)} %bitcast.15) | data formatting | bytes 33554432
  183.0 0.0 copy-start.3
  183.0 0.0 copy-start.2
  183.0 3.3 fusion.1
  186.3 0.8 copy.10
  187.1 0.0 all-gather.5.cloned.1.call-update
  187.1 0.0 reduce-scatter.2.cloned.1.call-start
  187.1 0.0 copy-done
  187.2 0.0 copy-done.3
  187.2 0.1 convert_bitcast_fusion
  187.3 0.0 copy-done.2
  187.3 7.4 %broadcast_add_fusion = s32[256,16,1024]{0,2,1:T(8,128)} fusion(s32[256,1024]{0,1:T(8,128)S(1)} %bitcast.17, s32[256,16]{0,1:T(8,128)S(1)} %dynamic-slice_bitcast_fusion), kind=kLoop, calls=%fused_computation.4 | loop fusion | flops 4194304 | bytes 17842176 | tf_op jit(solution)/shard_map/add | solution.py:14
  194.7 21.2 %fusion = bf16[256,16,1024,4]{0,3,2,1:T(4,128)(2,1)} fusion(s32[256,16,1024]{0,2,1:T(8,128)} %broadcast_add_fusion, bf16[256,1024]{0,1:T(8,128)(2,1)S(1)} %convert_bitcast_fusion), kind=kLoop, calls=%fused_computation.1 | loop fusion | flops 33554432 | bytes 50855936 | tf_op jit(solution)/shard_map/jit(_where)/select_n | solution.py:17
  215.9 46.5 %select_n.22 = bf16[256,65536]{0,1:T(8,128)(2,1)} reshape(bf16[256,16,1024,4]{0,3,2,1:T(4,128)(2,1)} %fusion) | data formatting | bytes 67108864 | tf_op jit(solution)/shard_map/jit(_where)/select_n | solution.py:17
  262.4 86.7 %all-gather.5.cloned.1.call-done = bf16[16,1024,512]{2,1,0:T(8,128)(2,1)} async-done(((bf16[16,16,512]{2,1,0:T(8,128)(2,1)}), bf16[16,1024,512]{2,1,0:T(8,128)(2,1)}) %all-gather.5.cloned.1.call-update) | async-done | bytes 16777232 | tf_op jit(solution)/shard_map/all_gather | solution.py:47
  349.0 26.6 %reshape.55 = bf16[65536,128]{1,0:T(8,128)(2,1)} reshape(bf16[16,1024,512]{2,1,0:T(8,128)(2,1)} %all-gather.5.cloned.1.call-done) | data formatting | bytes 33554432 | tf_op jit(solution)/shard_map/reshape | solution.py:47
  375.7 18.7 %convolution_multiply_fusion.1 = f32[256,128]{0,1:T(8,128)} fusion(bf16[256,65536]{0,1:T(8,128)(2,1)} %select_n.22, bf16[65536,128]{1,0:T(8,128)(2,1)} %reshape.55), kind=kOutput, calls=%fused_computation.5 | convolution fusion | flops 4295000064 | bytes 50462720 | tf_op jit(solution)/shard_map/dot_general | solution.py:45
  394.4 0.0 reduce-scatter.2.cloned.1.call-update
  394.4 35.7 %reduce-scatter.2.cloned.1.call-done = f32[256,32]{0,1:T(8,128)} async-done(((f32[256,128]{0,1:T(8,128)}), f32[256,32]{0,1:T(8,128)}) %reduce-scatter.2.cloned.1.call-update) | async-done | bytes 32784 | tf_op jit(solution)/shard_map/reduce_scatter | solution.py:51
  (3 shorter events, 0.0 us)
Async XLA Ops:
  6.5 180.6 %copy-start = (s32[16,16384]{1,0:T(8,128)S(1)}, s32[16,16384]{1,0:T(8,128)}, u32[]{:S(2)}) copy-start(s32[16,16384]{1,0:T(8,128)} %param.7) | copy-start | bytes 3145732
  6.5 160.6 %all-gather.3.cloned.1.call-start = ((), (), s32[]{:S(2)}) async-start(), calls=%async_computation.1 | async-start | bytes 20971520 | tf_op jit(solution)/shard_map/all_gather | solution.py:33
  7.3 341.8 %all-gather.5.cloned.1.call-start = ((), (), s32[]{:S(2)}) async-start(), calls=%async_computation.2 | async-start | bytes 17039360 | tf_op jit(solution)/shard_map/all_gather | solution.py:47
  183.0 4.2 copy-start.3
  183.0 4.3 copy-start.2
  187.1 243.1 %reduce-scatter.2.cloned.1.call-start = ((), (), s32[]{:S(2)}) async-start(), calls=%async_computation.3 | async-start | bytes 163840 | tf_op jit(solution)/shard_map/reduce_scatter | solution.py:51
  375.7 54.5 %copy-start.1 = (s32[16,16384]{1,0:T(8,128)S(1)}, s32[16,16384]{1,0:T(8,128)}, u32[]{:S(2)}) copy-start(s32[16,16384]{1,0:T(8,128)} %param.7) | copy-start | bytes 3145732
Sparse Core Ops, SparseCore 0:
  9.1 157.9 all-gather.2
  187.2 161.7 all-gather.4
  394.6 35.5 reduce-scatter.1
where the time goes:
time: 439 us; the launch traced here: 437 us
  waiting for transfers between devices  283 us (64%)
  local copies, waits for them, and re-layouts  89.8 us (20%)
  other arithmetic  28.7 us (7%)
  matrix products  22 us (5%)
  between operations  13.2 us (3%)
    all_gather x1, waiting for transfers between devices, on_device(): piece = lax.all_gather(encoded, 'tx', axis=0, tiled=True)  160 us
    all_gather x1, waiting for transfers between devices, on_device(): lax.all_gather(decoded, 'img', axis=1, tiled=True).reshape(-1, L)  86.7 us
    select_n x1, local copies, waits for them, and re-layouts, weights_for(): jnp.where(chosen, mask_rows.T[:, None, :, None].astype(jnp.bfloat16), jnp...  46.5 us
    reduce_scatter x1, waiting for transfers between devices, on_device(): lax.psum_scatter(image * scale, 'tx', scatter_dimension=1, tiled=True)  35.7 us
    reshape x1, local copies, waits for them, and re-layouts, on_device(): lax.all_gather(decoded, 'img', axis=1, tiled=True).reshape(-1, L)  26.6 us
    select_n x1, other arithmetic, weights_for(): jnp.where(chosen, mask_rows.T[:, None, :, None].astype(jnp.bfloat16), jnp...  21.2 us
    dot_general x1, matrix products, on_device(): jnp.dot(weight, lax.all_gather(decoded, 'img', axis=1, tiled=True).reshap...  18.7 us
    unnamed x10, local copies, waits for them, and re-layouts  16.7 us
  transfers between devices with their start and end apart: 3, of which 3 were waited for; matrix products, arithmetic and copies ran while one was open for 17% of the time, Pallas kernels for 0%

commit v1 on v0

--- a/solution.py
+++ b/solution.py
@@ -8,6 +8,13 @@
 K = 64
 R = 1024
 L = 128
+
+
+def all_by_exchange(x, name, along):
+    n_dev = lax.axis_size(name)
+    blocks = jnp.stack([x for _ in range(n_dev)])
+    blocks = lax.all_to_all(blocks, name, split_axis=0, concat_axis=0)
+    return jnp.concatenate(blocks, axis=along)
 
 
 def weights_for(rx_rows, mask_rows, tx_rows, block_count):
@@ -44,7 +51,7 @@
     weight = weights_for(rx_block, apodization, own_tx, block_count)
     image = jnp.dot(
         weight,
-        lax.all_gather(decoded, "img", axis=1, tiled=True).reshape(-1, L),
+        all_by_exchange(decoded, "img", 1).reshape(-1, L),
         preferred_element_type=jnp.float32,
     )
     scale = math.sqrt(E / (K * R))

time: 439 us -> 704 us (1.60)
  waiting for transfers between devices: 283 us -> 517 us
  local copies, waits for them, and re-layouts: 89.8 us -> 109 us
  starting transfers between devices: 0.08 us -> 12.1 us
    all_to_all x0 -> x1, waiting for transfers between devices: none -> 306 us  [all_by_exchange(): blocks = lax.all_to_all(blocks, name, split_axis=0, concat_axis=0)]
    all_gather x1 -> x0, waiting for transfers between devices: 86.7 us -> none  [on_device(): lax.all_gather(decoded, 'img', axis=1, tiled=True).reshape(-1, L)]
    another operation x0 -> x2, local copies, waits for them, and re-layouts: none -> 32.6 us  [the longest x1 26.6 us: on_device(): all_by_exchange(decoded, 'img', 1).reshape(-1, L)]
    reduce_scatter x1, waiting for transfers between devices: 35.7 us -> 51 us  [on_device(): lax.psum_scatter(image * scale, 'tx', scatter_dimension=1, tiled=True)]
    reshape x1, local copies, waits for them, and re-layouts: 26.6 us -> 14 us  [all_by_exchange(): return jnp.concatenate(blocks, axis=along)]
    all_to_all x0 -> x1, starting transfers between devices: none -> 12.1 us  [all_by_exchange(): blocks = lax.all_to_all(blocks, name, split_axis=0, concat_axis=0)]
  transfers between devices with their start and end apart: 3 -> 3, of which waited for: 3 -> 3; matrix products, arithmetic and copies ran while one was open for 17% -> 11% of each run, Pallas kernels for 0% -> 0%
where the time goes in v1:
time: 704 us; the launch traced here: 702 us
  waiting for transfers between devices  517 us (73%)
  local copies, waits for them, and re-layouts  109 us (15%)
  other arithmetic  28.7 us (4%)
  matrix products  21.9 us (3%)
  between operations  13.5 us (2%)
  starting transfers between devices  12.1 us (2%)
    all_to_all x1, waiting for transfers between devices, all_by_exchange(): blocks = lax.all_to_all(blocks, name, split_axis=0, concat_axis=0)  306 us
    all_gather x1, waiting for transfers between devices, on_device(): piece = lax.all_gather(encoded, 'tx', axis=0, tiled=True)  160 us
    reduce_scatter x1, waiting for transfers between devices, on_device(): lax.psum_scatter(image * scale, 'tx', scatter_dimension=1, tiled=True)  51 us
    select_n x1, local copies, waits for them, and re-layouts, weights_for(): jnp.where(chosen, mask_rows.T[:, None, :, None].astype(jnp.bfloat16), jnp...  46.2 us
    another operation x1, local copies, waits for them, and re-layouts, on_device(): all_by_exchange(decoded, 'img', 1).reshape(-1, L)  26.6 us
    select_n x1, other arithmetic, weights_for(): jnp.where(chosen, mask_rows.T[:, None, :, None].astype(jnp.bfloat16), jnp...  21.2 us
    dot_general x1, matrix products, on_device(): jnp.dot(weight, all_by_exchange(decoded, 'img', 1).reshape(-1, L), prefer...  18.7 us
    unnamed x10, local copies, waits for them, and re-layouts  15.9 us
  transfers between devices with their start and end apart: 3, of which 3 were waited for; matrix products, arithmetic and copies ran while one was open for 11% of the time, Pallas kernels for 0%

profile of v1, /device:TPU:1, one launch (start us, length us, event | category | flops | bytes accessed | tf_op | source)
XLA Modules:
  0.0 702.3 jit_solution(7112774801244619966)
XLA Ops:
  6.5 0.0 copy-start
  6.5 0.0 all-gather.2.cloned.1.call-start
  6.5 0.7 all-gather.2.cloned.1.call-update
  7.3 159.9 %all-gather.2.cloned.1.call-done = bf16[1024,16,512]{2,1,0:T(8,128)(2,1)} async-done(((bf16[256,16,512]{2,1,0:T(8,128)(2,1)}), bf16[1024,16,512]{2,1,0:T(8,128)(2,1)}) %all-gather.2.cloned.1.call-update) | async-done | bytes 16777232 | tf_op jit(solution)/shard_map/all_gather | solution.py:40
  167.1 15.8 %copy.10 = bf16[128,8,16,512]{3,1,2,0:T(8,128)(2,1)S(1)} copy(bf16[128,8,16,512]{3,2,1,0:T(8,128)(2,1)} %bitcast.18) | data formatting | bytes 33554432
  183.0 3.1 fusion.1
  186.1 0.1 copy.11
  186.2 6.0 stack.3
  192.2 12.1 %all-to-all-start = ((bf16[64,16,16,512]{3,2,1,0:T(8,128)(2,1)}), bf16[64,16,16,512]{3,2,1,0:T(8,128)(2,1)}, u32[]{:S(2)}, u32[]{:S(2)}) async-start(bf16[64,16,16,512]{3,2,1,0:T(8,128)(2,1)} %stack.3), calls=%async_computation | async-start | bytes 33554432 | tf_op jit(solution)/shard_map/all_to_all | solution.py:16
  204.3 0.0 reduce-scatter.2.cloned.1.call-start
  204.3 0.0 copy-done
  204.4 0.0 copy-done.3
  204.4 0.1 convert_bitcast_fusion
  204.5 0.0 copy-done.2
  204.5 7.4 %broadcast_add_fusion = s32[256,16,1024]{0,2,1:T(8,128)} fusion(s32[256,1024]{0,1:T(8,128)S(1)} %bitcast.21, s32[256,16]{0,1:T(8,128)S(1)} %dynamic-slice_bitcast_fusion), kind=kLoop, calls=%fused_computation.4 | loop fusion | flops 4194304 | bytes 17842176 | tf_op jit(solution)/shard_map/add | solution.py:21
  211.8 21.2 %fusion = bf16[256,16,1024,4]{0,3,2,1:T(4,128)(2,1)} fusion(s32[256,16,1024]{0,2,1:T(8,128)} %broadcast_add_fusion, bf16[256,1024]{0,1:T(8,128)(2,1)S(1)} %convert_bitcast_fusion), kind=kLoop, calls=%fused_computation.1 | loop fusion | flops 33554432 | bytes 50855936 | tf_op jit(solution)/shard_map/jit(_where)/select_n | solution.py:24
  233.1 46.2 %select_n.22 = bf16[256,65536]{0,1:T(8,128)(2,1)} reshape(bf16[256,16,1024,4]{0,3,2,1:T(4,128)(2,1)} %fusion) | data formatting | bytes 67108864 | tf_op jit(solution)/shard_map/jit(_where)/select_n | solution.py:24
  279.2 305.9 %all-to-all-done = bf16[64,16,16,512]{3,2,1,0:T(8,128)(2,1)} async-done(((bf16[64,16,16,512]{3,2,1,0:T(8,128)(2,1)}), bf16[64,16,16,512]{3,2,1,0:T(8,128)(2,1)}, u32[]{:S(2)}, u32[]{:S(2)}) %all-to-all-start) | async-done | bytes 16777248 | tf_op jit(solution)/shard_map/all_to_all | solution.py:16
  585.1 14.0 %copy.9 = bf16[16,64,16,512]{3,2,1,0:T(8,128)(2,1)} copy(bf16[16,64,16,512]{3,2,0,1:T(8,128)(2,1)} %bitcast.3) | data formatting | bytes 33554432 | tf_op jit(solution)/shard_map/reshape | solution.py:17
  599.1 26.6 %reshape_reshape.3 = bf16[65536,128]{1,0:T(8,128)(2,1)} reshape(bf16[16,64,16,512]{3,2,1,0:T(8,128)(2,1)} %copy.9) | data formatting | bytes 33554432 | tf_op jit(solution)/shard_map/reshape;reshape | solution.py:54
  625.7 18.7 %convolution_multiply_fusion.1 = f32[256,128]{0,1:T(8,128)} fusion(bf16[256,65536]{0,1:T(8,128)(2,1)} %select_n.22, bf16[65536,128]{1,0:T(8,128)(2,1)} %reshape_reshape.3), kind=kOutput, calls=%fused_computation.5 | convolution fusion | flops 4295000064 | bytes 50462720 | tf_op jit(solution)/shard_map/dot_general | solution.py:52
  644.4 0.0 reduce-scatter.2.cloned.1.call-update
  644.5 51.0 %reduce-scatter.2.cloned.1.call-done = f32[256,32]{0,1:T(8,128)} async-done(((f32[256,128]{0,1:T(8,128)}), f32[256,32]{0,1:T(8,128)}) %reduce-scatter.2.cloned.1.call-update) | async-done | bytes 32784 | tf_op jit(solution)/shard_map/reduce_scatter | solution.py:58
  695.5 0.0 copy-done.1
  (4 shorter events, 0.0 us)
Async XLA Ops:
  6.5 197.8 %copy-start = (s32[16,16384]{1,0:T(8,128)S(1)}, s32[16,16384]{1,0:T(8,128)}, u32[]{:S(2)}) copy-start(s32[16,16384]{1,0:T(8,128)} %param.7) | copy-start | bytes 3145732
  6.5 160.6 %all-gather.2.cloned.1.call-start = ((), (), s32[]{:S(2)}) async-start(), calls=%async_computation.2 | async-start | bytes 20971520 | tf_op jit(solution)/shard_map/all_gather | solution.py:40
  192.2 12.2 %copy-start.3 = (s32[1024,256]{1,0:T(8,128)S(1)}, s32[1024,256]{1,0:T(8,128)}, u32[]{:S(2)}) copy-start(s32[1024,256]{1,0:T(8,128)} %param.9) | copy-start | bytes 3145732
  192.2 12.3 %copy-start.2 = (s32[1024,256]{1,0:T(8,128)S(1)}, s32[1024,256]{1,0:T(8,128)}, u32[]{:S(2)}) copy-start(s32[1024,256]{1,0:T(8,128)} %param.8) | copy-start | bytes 3145732
  192.2 392.9 %all-to-all-start = ((bf16[64,16,16,512]{3,2,1,0:T(8,128)(2,1)}), bf16[64,16,16,512]{3,2,1,0:T(8,128)(2,1)}, u32[]{:S(2)}, u32[]{:S(2)}) async-start(bf16[64,16,16,512]{3,2,1,0:T(8,128)(2,1)} %stack.3), calls=%async_computation | async-start | bytes 33554432 | tf_op jit(solution)/shard_map/all_to_all | solution.py:16
  204.3 491.2 %reduce-scatter.2.cloned.1.call-start = ((), (), s32[]{:S(2)}) async-start(), calls=%async_computation.3 | async-start | bytes 163840 | tf_op jit(solution)/shard_map/reduce_scatter | solution.py:58
  625.7 69.8 %copy-start.1 = (s32[16,16384]{1,0:T(8,128)S(1)}, s32[16,16384]{1,0:T(8,128)}, u32[]{:S(2)}) copy-start(s32[16,16384]{1,0:T(8,128)} %param.7) | copy-start | bytes 3145732
Sparse Core Ops, SparseCore 0:
  9.1 157.9 all-gather.1
  644.6 50.8 reduce-scatter.1
